TPU v7x, 128 devices: a whole 4x4x4 slice. The times are simulated.
128 devices in a mesh: row: 16 (over z, x), col: 8 (over y, core).
Axes of the slice: x: 4, y: 4, z: 4, core: 2. Of those that a mesh axis runs over, the one named last changes fastest.
Arguments:
- tokens: bfloat16 [8192, 4096], P('row'), may hold values from -6 to 6
- theta: bfloat16 [96, 1024, 128], P('col', 'row'), may hold values from -0.1875 to 0.1875
- log_sigma2: float32 [96, 1024, 128], P('col', 'row'), may hold values from -8 to -5
- block_rows: int32 [96, 8], P('col'), may hold values from 0 to 31, as said below
- noise: bfloat16 [8192, 12288], P('row', 'col'), may hold values from -6 to 6
- cotangent: bfloat16 [8192, 12288], P('row', 'col'), may hold values from -6 to 6
Outputs:
- output: bfloat16 [8192, 12288], P('row', 'col')
- grad_tokens: float32 [8192, 4096], P('row', 'col')
- grad_theta: float32 [96, 1024, 128], P('col', 'row')
- grad_logvar: float32 [96, 1024, 128], P('col', 'row')
Inputs may be any that keep to these rules, and one draw needn't show every extreme that they name: `block_rows`: each row lists 8 distinct block rows in increasing order; row n contains n modulo 32, the others are drawn uniformly.
All inputs are finite; a program needn't handle non-finite values.
Results may differ from a plain program's by a relative error of at most 0.014.
Values may be sent and summed in bfloat16 or wider, within the bound.
No kernel may reach another device: no remote copies, remote signals or barrier semaphores. Data moves between devices by JAX's collectives and lax.ppermute only.
A program may use at most 192 MiB of HBM per device.

v0:
```python
import math

import jax
import jax.numpy as jnp
from jax import lax
from jax.sharding import Mesh
from jax.sharding import PartitionSpec as P

ROW = ("row_0", "row_1")


EPS = 1e-06


def side_by_side(arrays, axis, dim, along):
    both = jnp.concatenate(arrays, axis=along)
    out, at, finished = (lax.all_gather(both, axis, axis=dim, tiled=True), 0, [])
    for a in arrays:
        finished.append(lax.slice_in_dim(out, at, at + a.shape[along], axis=along))
        at += a.shape[along]
    return tuple(finished)


def summed_rows(shard, axes, dim):
    if not axes:
        return shard
    nearer = lax.psum_scatter(shard, axes[0], scatter_dimension=dim, tiled=True)
    return summed_rows(nearer, axes[1:], dim)


def cut_along(shard, dim, count):
    lengths = shard.shape
    blocks = shard.reshape(*lengths[:dim], count, lengths[dim] // count, *lengths[dim + 1 :])
    return jnp.moveaxis(blocks, dim, 0)


def sent_and_summed(shard, axis, dim):
    blocks = cut_along(shard, dim, lax.axis_size(axis))
    arrived = lax.all_to_all(blocks, axis, split_axis=0, concat_axis=0, tiled=True)
    return arrived.astype(jnp.float32).sum(axis=0)


def squares_of(values):
    wide = values.astype(jnp.float32)
    return (wide * wide).astype(jnp.bfloat16)


def body(tokens, theta, log_sigma2, block_rows, noise, cotangent):
    sigma = jnp.exp(log_sigma2)
    sigma_low = sigma.astype(jnp.bfloat16)
    tok_rows = tokens.shape[0]
    blk = theta.shape[2]
    columns = theta.shape[0]
    kblocks = tokens.shape[1] // blk
    width = block_rows.shape[1] * blk
    tiles = tokens.reshape(tok_rows, kblocks, blk)
    flat_rows = block_rows.reshape(-1)
    panel = jnp.take(tiles, flat_rows, axis=1).reshape(tok_rows, columns, width)
    sq_panel = squares_of(panel)
    whole_theta, whole_sigma = side_by_side((theta, sigma_low), ROW, 1, 0)
    mean_out = jnp.einsum("tnk,nkj->tnj", panel, whole_theta, preferred_element_type=jnp.float32)
    var_out = jnp.einsum("tnk,nkj->tnj", sq_panel, whole_sigma, preferred_element_type=jnp.float32)
    mean_out = mean_out.reshape(tok_rows, columns * blk)
    var_out = var_out.reshape(tok_rows, columns * blk)
    root = jnp.sqrt(var_out + EPS)
    draw = noise.astype(jnp.float32)
    output = (mean_out + root * draw).astype(jnp.bfloat16)
    grad_var = (cotangent.astype(jnp.float32) * draw / (2.0 * root)).astype(jnp.bfloat16)
    cot_blocks = cotangent.reshape(tok_rows, columns, blk)
    var_blocks = grad_var.reshape(tok_rows, columns, blk)
    part_theta = jnp.einsum("tnk,tnj->nkj", panel, cot_blocks, preferred_element_type=jnp.float32)
    part_var = jnp.einsum("tnk,tnj->nkj", sq_panel, var_blocks, preferred_element_type=jnp.float32)
    low_theta, low_var = lax.optimization_barrier(
        (part_theta.astype(jnp.bfloat16), part_var.astype(jnp.bfloat16))
    )
    sum_theta, sum_var = (
        summed_rows(low_theta.astype(jnp.float32).astype(jnp.bfloat16), ROW, 1).astype(jnp.float32),
        summed_rows(low_var.astype(jnp.float32).astype(jnp.bfloat16), ROW, 1).astype(jnp.float32),
    )
    total_tokens = tok_rows * lax.axis_size(ROW)
    grad_theta = sum_theta * (1.0 / math.sqrt(total_tokens))
    grad_logvar = sigma * sum_var * (width / math.sqrt(total_tokens))
    first = jnp.einsum("tnj,nkj->tnk", cot_blocks, whole_theta, preferred_element_type=jnp.float32)
    second = jnp.einsum("tnj,nkj->tnk", var_blocks, whole_sigma, preferred_element_type=jnp.float32)
    back_panel = first + 2.0 * panel.astype(jnp.float32) * second
    spread_back = jnp.zeros((tok_rows, kblocks, blk), jnp.float32)
    spread_back = spread_back.at[:, flat_rows].add(
        back_panel.reshape(tok_rows, columns * block_rows.shape[1], blk)
    )
    low_back = lax.optimization_barrier(
        spread_back.reshape(tok_rows, kblocks * blk).astype(jnp.bfloat16)
    )
    grad_tokens = sent_and_summed(low_back.astype(jnp.float32).astype(jnp.bfloat16), "col", 1)
    return (output, grad_tokens, grad_theta, grad_logvar)


def solution(mesh):
    finer = Mesh(mesh.devices.reshape(4, 4, mesh.shape["col"]), ("row_0", "row_1", "col"))
    in_specs = (
        P(ROW, None),
        P("col", ROW, None),
        P("col", ROW, None),
        P("col", None),
        P(ROW, "col"),
        P(ROW, "col"),
    )
    out_specs = (P(ROW, "col"), P(ROW, "col"), P("col", ROW, None), P("col", ROW, None))
    return jax.shard_map(body, mesh=finer, in_specs=in_specs, out_specs=out_specs, check_vma=False)
```

profile of v0, /device:TPU:1, one launch (start us, length us, event | category | flops | bytes accessed | tf_op | source)
XLA Modules:
  0.0 329.6 jit_solution(5350106335574732727)
XLA Ops:
  7.2 0.0 all-gather.2.cloned.1.call-start
  7.2 1.1 copy.73
  8.3 1.3 fusion.17
  9.6 0.9 pad_maximum_fusion
  10.5 0.0 reduce-scatter.9.cloned.1.call-start
  10.5 0.8 copy.77
  11.3 0.1 reshape.75
  11.4 6.5 %copy.76 = bf16[512,4096]{0,1:T(8,128)(2,1)} copy(bf16[512,4096]{1,0:T(8,128)(2,1)} %param.6) | data formatting | bytes 8388608 | tf_op args[0]
  17.9 6.4 %copy.78 = bf16[512,32,128]{2,0,1:T(8,128)(2,1)} copy(bf16[512,32,128]{0,2,1:T(8,128)(2,1)} %bitcast.48) | data formatting | bytes 8388608 | tf_op jit(solution)/shard_map/reshape | solution.py:56
  24.3 9.2 %gather_fusion = bf16[96,512,128]{2,1,0:T(8,128)(2,1)} fusion(bf16[512,32,128]{2,0,1:T(8,128)(2,1)} %copy.78, s32[1024]{0:T(1024)S(1)} %pad_clamp_fusion), kind=kCustom, calls=%fused_computation | custom fusion | bytes 25166208 | tf_op jit(solution)/shard_map/jit(_take)/gather | solution.py:58
  33.4 16.0 %copy.79 = bf16[512,96,128]{0,2,1:T(8,128)(2,1)} copy(bf16[512,96,128]{2,0,1:T(8,128)(2,1)} %bitcast.46) | data formatting | bytes 25165824 | tf_op jit(solution)/shard_map/jit(_take)/gather | solution.py:58
  49.4 0.1 copy.75
  49.5 0.1 broadcast_in_dim.18
  49.6 1.7 copy.84
  51.4 3.2 copy.83
  54.5 6.9 %bitcast_select_fusion = bf16[512,12,1024]{0,2,1:T(8,128)(2,1)S(1)} fusion(pred[12,1024]{1,0:T(8,128)(4,1)S(1)} %bitcast.54, bf16[512,12,1024]{0,2,1:T(8,128)(2,1)} %bitcast.45), kind=kLoop, calls=%fused_computation.7 | loop fusion | flops 6291456 | bytes 25178112 | tf_op jit(solution)/shard_map/jit(_take)/select_n | solution.py:58
  61.5 4.6 %copy-done = bf16[512,12,1024]{0,2,1:T(8,128)(2,1)} copy-done((bf16[512,12,1024]{0,2,1:T(8,128)(2,1)}, bf16[512,12,1024]{0,2,1:T(8,128)(2,1)S(1)}, u32[]{:S(2)}) %copy-start) | copy-done | bytes 12582936
  66.1 4.7 %convolution_convert_fusion = bf16[12,1024,128]{2,1,0:T(8,128)(2,1)} fusion(bf16[512,12,1024]{0,2,1:T(8,128)(2,1)S(1)} %bitcast_select_fusion, bf16[512,12,128]{0,2,1:T(8,128)(2,1)S(1)} %bitcast.49), kind=kOutput, calls=%fused_computation.20 | convolution fusion | flops 1612185600 | bytes 17301504 | tf_op jit(solution)/shard_map/tnk,tnj->nkj/dot_general | solution.py:71
  70.8 4.4 %all-gather.2.cloned.1.call-done = bf16[24,1024,128]{2,0,1:T(8,128)(2,1)} async-done(((bf16[24,64,128]{2,0,1:T(8,128)(2,1)}), bf16[24,1024,128]{2,0,1:T(8,128)(2,1)}) %all-gather.2.cloned.1.call-update) | async-done | bytes 6291472 | tf_op jit(solution)/shard_map/all_gather | solution.py:17
  75.2 6.3 %fusion.20 = (bf16[12,1024,128]{2,0,1:T(8,128)(2,1)}, bf16[12,1024,128]{2,0,1:T(8,128)(2,1)}) fusion(bf16[24,1024,128]{2,0,1:T(8,128)(2,1)} %all-gather.2.cloned.1.call-done), kind=kLoop, calls=%fused_computation.32 | loop fusion | bytes 12582912 | tf_op jit(solution)/shard_map/slice | solution.py:19
  81.5 7.9 %copy.107 = bf16[12,1024,128]{1,2,0:T(8,128)(2,1)S(1)} copy(bf16[12,1024,128]{2,0,1:T(8,128)(2,1)} %get-tuple-element.24) | data formatting | bytes 6291456
  89.4 10.7 %add_sqrt_fusion = f32[12,128,512]{2,1,0:T(8,128)} fusion(bf16[12,1024,128]{1,2,0:T(8,128)(2,1)S(1)} %copy.107, bf16[512,12,1024]{0,2,1:T(8,128)(2,1)} %copy-done), kind=kOutput, calls=%fused_computation.18 | convolution fusion | flops 1630273536 | bytes 18874368 | tf_op jit(solution)/shard_map/tnk,nkj->tnj/dot_general | solution.py:62
  100.1 8.1 %copy.106 = bf16[12,1024,128]{1,2,0:T(8,128)(2,1)S(1)} copy(bf16[12,1024,128]{2,0,1:T(8,128)(2,1)} %get-tuple-element.25) | data formatting | bytes 6291456
  108.3 6.5 %fusion.21 = f32[12,128,512]{2,1,0:T(8,128)S(1)} fusion(bf16[12,1024,128]{1,2,0:T(8,128)(2,1)S(1)} %copy.106, bf16[512,12,1024]{0,2,1:T(8,128)(2,1)} %copy-done), kind=kOutput, calls=%fused_computation.33 | convolution fusion | flops 1610612736 | bytes 18874368 | tf_op jit(solution)/shard_map/tnk,nkj->tnj/dot_general | solution.py:61
  114.9 2.4 fusion.10
  117.3 1.2 copy-done.5
  118.5 9.7 %fusion.11 = bf16[12,1024,128]{2,1,0:T(8,128)(2,1)} fusion(bf16[512,12,128]{0,2,1:T(8,128)(2,1)S(1)} %bitcast.51, bf16[512,12,1024]{0,2,1:T(8,128)(2,1)} %copy-done), kind=kOutput, calls=%fused_computation.19 | convolution fusion | flops 1631059968 | bytes 17301504 | tf_op jit(solution)/shard_map/tnk,tnj->nkj/dot_general | solution.py:72
  128.2 0.0 reduce-scatter.5.cloned.1.call-start
  128.2 0.7 reduce-scatter.5.cloned.1.call-update
  128.9 12.3 %fusion.22 = f32[12,1024,512]{2,1,0:T(8,128)} fusion(bf16[12,1024,128]{1,2,0:T(8,128)(2,1)S(1)} %copy.106, bf16[512,12,128]{0,2,1:T(8,128)(2,1)} %bitcast.50), kind=kOutput, calls=%fused_computation.34 | convolution fusion | flops 1610612736 | bytes 29884416 | tf_op jit(solution)/shard_map/tnj,nkj->tnk/dot_general | solution.py:83
  141.2 22.8 %fusion.2 = f32[512,12,1024]{0,2,1:T(8,128)} fusion(bf16[512,12,1024]{0,2,1:T(8,128)(2,1)} %copy-done, f32[12,1024,512]{2,1,0:T(8,128)} %fusion.22, bf16[12,1024,128]{1,2,0:T(8,128)(2,1)S(1)} %copy-done.2, bf16[512,12,128]{0,2,1:T(8,128)(2,1)S(1)} %bitcast.52), kind=kOutput, calls=%fused_computation.6 | convolution fusion | flops 1635778560 | bytes 67633152 | tf_op jit(solution)/shard_map/tnj,nkj->tnk/dot_general | solution.py:84
  164.1 24.6 %copy.90 = f32[512,96,128]{2,0,1:T(8,128)} copy(f32[512,96,128]{0,2,1:T(8,128)} %bitcast.43) | data formatting | bytes 50331648 | tf_op jit(solution)/shard_map/reshape | solution.py:88
  188.7 4.2 %broadcast_in_dim.22 = f32[512,32,128]{2,0,1:T(8,128)} broadcast(f32[]{:T(128)} %constant.14.clone.1), dimensions={} | broadcast | bytes 8388612 | tf_op jit(solution)/shard_map/broadcast_in_dim | solution.py:86
  192.9 55.6 %scatter_fusion = f32[512,32,128]{2,0,1:T(8,128)} fusion(f32[512,32,128]{2,0,1:T(8,128)} %broadcast_in_dim.22, s32[96]{0:T(128)S(1)} %fusion.19, f32[96,512,128]{2,1,0:T(8,128)} %bitcast.44), kind=kCustom, calls=%fused_computation.1 | custom fusion | flops 6291456 | bytes 75497856 | tf_op jit(solution)/shard_map/scatter-add | solution.py:87
  248.5 6.0 %convert_element_type.56 = bf16[512,32,128]{2,0,1:T(8,128)(2,1)} convert(f32[512,32,128]{2,0,1:T(8,128)} %scatter_fusion) | non-fusion elementwise | flops 2097152 | bytes 12582912 | tf_op jit(solution)/shard_map/convert_element_type | solution.py:91
  254.5 6.5 %copy.91 = bf16[512,32,128]{0,2,1:T(8,128)(2,1)} copy(bf16[512,32,128]{2,0,1:T(8,128)(2,1)} %convert_element_type.56) | data formatting | bytes 8388608 | tf_op jit(solution)/shard_map/convert_element_type | solution.py:91
  260.9 5.3 %all-to-all-start = ((bf16[8,512,512]{1,2,0:T(8,128)(2,1)}), bf16[8,512,512]{1,2,0:T(8,128)(2,1)}, u32[]{:S(2)}, u32[]{:S(2)}) async-start(bf16[8,512,512]{1,2,0:T(8,128)(2,1)} %bitcast.47), calls=%async_computation | async-start | bytes 8388608 | tf_op jit(solution)/shard_map/all_to_all | solution.py:39
  266.3 2.7 copy.94
  269.0 0.0 reduce-scatter.7.cloned.1.call-start
  269.1 0.0 reduce-scatter.5.cloned.1.call-done
  269.1 0.5 reduce-scatter.7.cloned.1.call-update
  269.6 1.6 copy.95
  271.2 43.9 %all-to-all-done = bf16[8,512,512]{1,2,0:T(8,128)(2,1)} async-done(((bf16[8,512,512]{1,2,0:T(8,128)(2,1)}), bf16[8,512,512]{1,2,0:T(8,128)(2,1)}, u32[]{:S(2)}, u32[]{:S(2)}) %all-to-all-start) | async-done | bytes 4194336 | tf_op jit(solution)/shard_map/all_to_all | solution.py:39
  315.1 2.9 convert_reduce_fusion
  318.0 1.3 copy.96
  319.3 1.3 fusion.18
  320.5 0.9 copy.97
  321.4 1.7 convert_multiply_fusion.4
  (34 shorter events, 0.1 us)
Async XLA Ops:
  7.2 68.0 %all-gather.2.cloned.1.call-start = ((), (), s32[]{:S(2)}) async-start(), calls=%async_computation.5 | async-start | bytes 6684672 | tf_op jit(solution)/shard_map/all_gather | solution.py:17
  10.5 255.8 %reduce-scatter.9.cloned.1.call-start = ((), (), s32[]{:S(2)}) async-start(), calls=%async_computation.8 | async-start | bytes 3932160 | tf_op jit(solution)/shard_map/reduce_scatter | solution.py:27
  33.4 16.0 %copy-start.11 = (s32[12,8]{0,1:T(8,128)S(1)}, s32[12,8]{0,1:T(8,128)}, u32[]{:S(2)}) copy-start(s32[12,8]{0,1:T(8,128)} %param.9) | copy-start | bytes 1156
  51.4 10.1 %copy-start.3 = (bf16[512,1536]{0,1:T(8,128)(2,1)}, bf16[512,1536]{0,1:T(8,128)(2,1)S(1)}, u32[]{:S(2)}) copy-start(bf16[512,1536]{0,1:T(8,128)(2,1)S(1)} %copy.84) | copy-start | bytes 4718596
  61.5 4.6 %copy-start = (bf16[512,12,1024]{0,2,1:T(8,128)(2,1)}, bf16[512,12,1024]{0,2,1:T(8,128)(2,1)S(1)}, u32[]{:S(2)}) copy-start(bf16[512,12,1024]{0,2,1:T(8,128)(2,1)S(1)} %bitcast_select_fusion) | copy-start | bytes 37748740
  89.4 10.7 %copy-start.1 = (bf16[12,1024,128]{1,2,0:T(8,128)(2,1)}, bf16[12,1024,128]{1,2,0:T(8,128)(2,1)S(1)}, u32[]{:S(2)}) copy-start(bf16[12,1024,128]{1,2,0:T(8,128)(2,1)S(1)} %copy.107) | copy-start | bytes 9437188
  108.3 6.6 %copy-start.4 = (bf16[512,1536]{0,1:T(8,128)(2,1)S(1)}, bf16[512,1536]{0,1:T(8,128)(2,1)}, u32[]{:S(2)}) copy-start(bf16[512,1536]{0,1:T(8,128)(2,1)} %copy-done.3) | copy-start | bytes 4718596
  108.3 6.6 %copy-start.8 = (bf16[512,1536]{0,1:T(8,128)(2,1)S(1)}, bf16[512,1536]{0,1:T(8,128)(2,1)}, u32[]{:S(2)}) copy-start(bf16[512,1536]{0,1:T(8,128)(2,1)} %copy.83) | copy-start | bytes 4718596
  108.3 6.6 %copy-start.9 = (f32[12,128,512]{2,1,0:T(8,128)S(1)}, f32[12,128,512]{2,1,0:T(8,128)}, u32[]{:S(2)}) copy-start(f32[12,128,512]{2,1,0:T(8,128)} %add_sqrt_fusion) | copy-start | bytes 9437188
  117.3 1.2 copy-start.5
  128.2 140.9 %reduce-scatter.5.cloned.1.call-start = ((), (), s32[]{:S(2)}) async-start(), calls=%async_computation.6 | async-start | bytes 3932160 | tf_op jit(solution)/shard_map/reduce_scatter | solution.py:27
  128.9 12.3 %copy-start.2 = (bf16[12,1024,128]{1,2,0:T(8,128)(2,1)S(1)}, bf16[12,1024,128]{1,2,0:T(8,128)(2,1)}, u32[]{:S(2)}) copy-start(bf16[12,1024,128]{1,2,0:T(8,128)(2,1)} %copy-done.1) | copy-start | bytes 9437188
  128.9 12.3 %copy-start.6 = (bf16[512,1536]{0,1:T(8,128)(2,1)S(1)}, bf16[512,1536]{0,1:T(8,128)(2,1)}, u32[]{:S(2)}) copy-start(bf16[512,1536]{0,1:T(8,128)(2,1)} %copy-done.5) | copy-start | bytes 4718596
  260.9 8.7 %copy-start.7 = (bf16[512,1536]{0,1:T(8,128)(2,1)S(1)}, bf16[512,1536]{0,1:T(8,128)(2,1)}, u32[]{:S(2)}) copy-start(bf16[512,1536]{0,1:T(8,128)(2,1)} %get-tuple-element.27) | copy-start | bytes 4718596
  260.9 54.1 %all-to-all-start = ((bf16[8,512,512]{1,2,0:T(8,128)(2,1)}), bf16[8,512,512]{1,2,0:T(8,128)(2,1)}, u32[]{:S(2)}, u32[]{:S(2)}) async-start(bf16[8,512,512]{1,2,0:T(8,128)(2,1)} %bitcast.47), calls=%async_computation | async-start | bytes 8388608 | tf_op jit(solution)/shard_map/all_to_all | solution.py:39
  266.3 53.0 %reduce-scatter.11.cloned.1.call-start = ((), (), s32[]{:S(2)}) async-start(), calls=%async_computation.9 | async-start | bytes 1310720 | tf_op jit(solution)/shard_map/reduce_scatter | solution.py:27
  269.0 52.4 %reduce-scatter.7.cloned.1.call-start = ((), (), s32[]{:S(2)}) async-start(), calls=%async_computation.7 | async-start | bytes 983040 | tf_op jit(solution)/shard_map/reduce_scatter | solution.py:27
  271.2 48.1 %copy-start.10 = (f32[12,64,128]{2,1,0:T(8,128)S(1)}, f32[12,64,128]{2,1,0:T(8,128)}, u32[]{:S(2)}) copy-start(f32[12,64,128]{2,1,0:T(8,128)} %param.8) | copy-start | bytes 1179652
Sparse Core Ops, SparseCore 0:
  10.7 64.4 all-gather.1
  128.3 38.1 reduce-scatter.8
  168.9 38.0 reduce-scatter.4
  269.2 21.7 reduce-scatter.10
  293.2 22.0 reduce-scatter.6
where the time goes:
time: 332 us; the launch traced here: 330 us
  local copies, waits for them, and re-layouts  115 us (35%)
  other arithmetic  78.9 us (24%)
  matrix products  66.7 us (20%)
  waiting for transfers between devices  49.5 us (15%)
  between operations  14 us (4%)
  starting transfers between devices  5.47 us (2%)
    scatter-add x1, other arithmetic, body(): spread_back.at[:, flat_rows]  55.6 us
    all_to_all x1, waiting for transfers between devices, sent_and_summed(): lax.all_to_all(blocks, axis, split_axis=0, concat_axis=0, tiled=True)  43.9 us
    unnamed x36, local copies, waits for them, and re-layouts  38.9 us
    gather x2, local copies, waits for them, and re-layouts, body(): panel = jnp.take(tiles, flat_rows, axis=1).reshape(tok_rows, columns, width)  25.1 us
    reshape x1, local copies, waits for them, and re-layouts, body(): back_panel.reshape(tok_rows, columns * block_rows.shape[1], blk)  24.6 us
    dot_general x1, matrix products, body(): jnp.einsum('tnj,nkj->tnk', var_blocks, whole_sigma, preferred_element_typ...  22.8 us
    dot_general x1, matrix products, body(): jnp.einsum('tnj,nkj->tnk', cot_blocks, whole_theta, preferred_element_typ...  12.3 us
    dot_general x1, matrix products, body(): jnp.einsum('tnk,nkj->tnj', sq_panel, whole_sigma, preferred_element_type=...  10.7 us
  transfers between devices with their start and end apart: 6, of which 2 were waited for; matrix products, arithmetic and copies ran while one was open for 60% of the time, Pallas kernels for 0%

commit v1 on v0

v1 whole, which is shorter than its diff:
```python
import math
import jax, jax.numpy as jnp
from jax import lax
from jax.experimental import pallas as pl
from jax.experimental.pallas import tpu as pltpu
from jax.sharding import Mesh
from jax.sharding import PartitionSpec as P

ROW = ("row_0", "row_1")

EPS = 1e-06
VM = pltpu.CompilerParams(vmem_limit_bytes=60 * 1024 * 1024)
f32, bf16 = jnp.float32, jnp.bfloat16

def lanes(ref, index, rows=slice(None)):
    return ref[rows, pl.ds(pl.multiple_of(index * 128, 128), 128)]

def tiles_of(ref, rows_ref, n, count):
    return [ref.at[:, pl.ds(pl.multiple_of(rows_ref[n, s] * 128, 128), 128)] for s in range(count)]

def prep_kernel(theta_ref, ls_ref, th_ref, sg_ref):
    for n in range(theta_ref.shape[0]):
        th_ref[:, n * 128:(n + 1) * 128] = theta_ref[n]
        sg_ref[:, n * 128:(n + 1) * 128] = jnp.exp(ls_ref[n]).astype(bf16)

def prep(theta, ls):
    c, r, b = theta.shape
    o = jax.ShapeDtypeStruct((r, c * b), bf16)
    return pl.pallas_call(prep_kernel, out_shape=(o, o), compiler_params=VM, name="prep")(theta, ls)

def k1_kernel(rows_ref, tok_ref, cot_ref, part_ref, tokT_ref):
    kb = tok_ref.shape[1] // 128
    cols = cot_ref.shape[1] // 128
    ks = rows_ref.shape[1]
    for k in range(kb):
        tokT_ref[k] = tok_ref[:, k * 128:(k + 1) * 128].T
    def step(n, _):
        lhs = jnp.concatenate([tokT_ref[rows_ref[n, s]] for s in range(ks)], axis=0)
        part = jnp.dot(lhs, lanes(cot_ref, n), preferred_element_type=f32)
        part_ref[:, pl.ds(pl.multiple_of(n * 128, 128), 128)] = part.astype(bf16)
        return 0
    lax.fori_loop(0, cols, step, 0)

SM = pl.BlockSpec(memory_space=pltpu.SMEM)
VB = pl.BlockSpec(memory_space=pltpu.VMEM)

def k1(rows, tok, cot):
    t, d = tok.shape
    width = rows.shape[1] * 128
    return pl.pallas_call(k1_kernel,
        out_shape=(jax.ShapeDtypeStruct((width, cot.shape[1]), bf16), jax.ShapeDtypeStruct((d // 128, 128, t), bf16)),
        in_specs=[SM, VB, VB], out_specs=(VB, VB), compiler_params=VM, name="k1")(rows, tok, cot)

def k2_kernel(rows_ref, tok_ref, tokT_ref, sg_ref, noise_ref, cot_ref, part_ref, gv_ref, rn_ref, sq_ref, sqT_ref):
    kb = tok_ref.shape[1] // 128
    cols = cot_ref.shape[1] // 128
    ks = rows_ref.shape[1]
    for k in range(kb):
        w = tok_ref[:, k * 128:(k + 1) * 128].astype(f32)
        sq_ref[:, k * 128:(k + 1) * 128] = (w * w).astype(bf16)
        w = tokT_ref[k].astype(f32)
        sqT_ref[k] = (w * w).astype(bf16)
    def step(n, _):
        at = pl.ds(pl.multiple_of(n * 128, 128), 128)
        lhs = jnp.concatenate([lanes(sq_ref, rows_ref[n, s]) for s in range(ks)], axis=1)
        var = jnp.dot(lhs, sg_ref[:, at], preferred_element_type=f32)
        root = jnp.sqrt(var + EPS)
        draw = noise_ref[:, at].astype(f32)
        rn_ref[:, at] = root * draw
        gv = (cot_ref[:, at].astype(f32) * draw / (2.0 * root)).astype(bf16)
        gv_ref[:, at] = gv
        lhs = jnp.concatenate([sqT_ref[rows_ref[n, s]] for s in range(ks)], axis=0)
        part = jnp.dot(lhs, gv, preferred_element_type=f32)
        part_ref[:, at] = part.astype(bf16)
        return 0
    lax.fori_loop(0, cols, step, 0)

def k2(rows, tok, tokT, sg, noise, cot):
    t, d = tok.shape
    width, ff = sg.shape
    return pl.pallas_call(k2_kernel,
        out_shape=(jax.ShapeDtypeStruct((width, ff), bf16), jax.ShapeDtypeStruct((t, ff), bf16), jax.ShapeDtypeStruct((t, ff), f32)),
        in_specs=[SM, VB, VB, VB, VB, VB], out_specs=(VB, VB, VB),
        scratch_shapes=[pltpu.VMEM((t, d), bf16), pltpu.VMEM((d // 128, 128, t), bf16)],
        compiler_params=VM, name="k2")(rows, tok, tokT, sg, noise, cot)

NT = (((1,), (1,)), ((), ()))

def k3_kernel(rows_ref, tok_ref, th_ref, sg_ref, cot_ref, gv_ref, rn_ref, out_ref, dx_ref, acc_ref):
    t = tok_ref.shape[0]
    kb = tok_ref.shape[1] // 128
    cols = cot_ref.shape[1] // 128
    ks = rows_ref.shape[1]
    acc_ref[...] = jnp.zeros_like(acc_ref)
    def step(n, _):
        at = pl.ds(pl.multiple_of(n * 128, 128), 128)
        th = th_ref[:, at]
        sg = sg_ref[:, at]
        lhs = jnp.concatenate([lanes(tok_ref, rows_ref[n, s]) for s in range(ks)], axis=1)
        mean = jnp.dot(lhs, th, preferred_element_type=f32)
        out_ref[:, at] = (mean + rn_ref[:, at]).astype(bf16)
        cot = cot_ref[:, at]
        gv = gv_ref[:, at]
        first = lax.dot_general(cot, th, NT, preferred_element_type=f32)
        second = lax.dot_general(gv, sg, NT, preferred_element_type=f32)
        for s in range(ks):
            pick = pl.ds(pl.multiple_of(rows_ref[n, s] * 128, 128), 128)
            p = slice(s * 128, (s + 1) * 128)
            acc_ref[:, pick] += first[:, p] + 2.0 * tok_ref[:, pick].astype(f32) * second[:, p]
        return 0
    lax.fori_loop(0, cols, step, 0)
    w = dx_ref.shape[2]
    for c in range(dx_ref.shape[0]):
        dx_ref[c] = acc_ref[:, c * w:(c + 1) * w].astype(bf16)

def k3(rows, tok, th, sg, cot, gv, rn):
    t, d = tok.shape
    ff = cot.shape[1]
    return pl.pallas_call(k3_kernel,
        out_shape=(jax.ShapeDtypeStruct((t, ff), bf16), jax.ShapeDtypeStruct((8, t, d // 8), bf16)),
        in_specs=[SM, VB, VB, VB, VB, VB, VB], out_specs=(VB, VB),
        scratch_shapes=[pltpu.VMEM((t, d), f32)],
        compiler_params=VM, name="k3")(rows, tok, th, sg, cot, gv, rn)


def body(tokens, theta, log_sigma2, block_rows, noise, cotangent):
    th_own, sg_own = prep(theta, log_sigma2)
    sg = lax.all_gather(sg_own, ROW, axis=0, tiled=True)
    th = lax.all_gather(th_own, ROW, axis=0, tiled=True)
    part_theta, tokT = k1(block_rows, tokens, cotangent)
    part_var, gv, rn = k2(block_rows, tokens, tokT, sg, noise, cotangent)
    output, dx = k3(block_rows, tokens, th, sg, cotangent, gv, rn)
    sum_theta = lax.psum_scatter(part_theta, ROW, scatter_dimension=0, tiled=True).astype(f32)
    sum_var = lax.psum_scatter(part_var, ROW, scatter_dimension=0, tiled=True).astype(f32)
    c, r, b = theta.shape
    width = part_theta.shape[0]
    tokens_all = tokens.shape[0] * lax.axis_size(ROW)
    back = lambda v: v.reshape(r, c, b).transpose(1, 0, 2)
    grad_theta = back(sum_theta) * (1.0 / math.sqrt(tokens_all))
    grad_logvar = jnp.exp(log_sigma2) * back(sum_var) * (width / math.sqrt(tokens_all))
    arrived = lax.all_to_all(dx, "col", split_axis=0, concat_axis=0, tiled=True)
    grad_tokens = arrived.astype(f32).sum(axis=0)
    return (output, grad_tokens, grad_theta, grad_logvar)


def solution(mesh):
    finer = Mesh(mesh.devices.reshape(4, 4, mesh.shape["col"]), ("row_0", "row_1", "col"))
    in_specs = (P(ROW, None), P("col", ROW, None), P("col", ROW, None), P("col", None), P(ROW, "col"), P(ROW, "col"))
    out_specs = (P(ROW, "col"), P(ROW, "col"), P("col", ROW, None), P("col", ROW, None))
    return jax.shard_map(body, mesh=finer, in_specs=in_specs, out_specs=out_specs, check_vma=False)
```

time: 332 us -> 278 us (0.84)
  waiting for transfers between devices: 49.5 us -> 180 us
  local copies, waits for them, and re-layouts: 115 us -> 4.23 us
  other arithmetic: 78.9 us -> 5.11 us
  Pallas kernels: 0 us -> 66.9 us
  matrix products: 66.7 us -> 0 us
    reduce_scatter x4 -> x2, waiting for transfers between devices: 0.02 us -> 115 us  [the longest x1 70.8 us: body(): lax.psum_scatter(part_var, ROW, scatter_dimension=0, tiled=True).astype(f32)]
    pallas_call x0 -> x4, Pallas kernels: none -> 66.9 us  [the longest x1 27.7 us: k3(): pl.pallas_call(k3_kernel, out_shape=(jax.ShapeDtypeStruct((t, ff), bf16),...]
    dot_general x6 -> x0, matrix products: 66.7 us -> none  [the longest x1 22.8 us: body(): jnp.einsum('tnj,nkj->tnk', var_blocks, whole_sigma, preferred_element_typ...]
    all_gather x1 -> x2, waiting for transfers between devices: 4.37 us -> 61.8 us  [the longest x1 38.2 us: body(): sg = lax.all_gather(sg_own, ROW, axis=0, tiled=True)]
    scatter-add x1 -> x0, other arithmetic: 55.6 us -> none  [body(): spread_back.at[:, flat_rows]]
    all_to_all x1, waiting for transfers between devices: 43.9 us -> 2.29 us  [body(): arrived = lax.all_to_all(dx, 'col', split_axis=0, concat_axis=0, tiled=True)]
    unnamed x36 -> x5, local copies, waits for them, and re-layouts: 38.9 us -> 3.1 us
    reshape x3 -> x0, local copies, waits for them, and re-layouts: 31.1 us -> none  [the longest x1 24.6 us: body(): back_panel.reshape(tok_rows, columns * block_rows.shape[1], blk)]
  transfers between devices with their start and end apart: 6 -> 5, of which waited for: 2 -> 5; matrix products, arithmetic and copies ran while one was open for 60% -> 3% of each run, Pallas kernels for 0% -> 24%
where the time goes in v1:
time: 278 us; the launch traced here: 276 us
  waiting for transfers between devices  180 us (65%)
  Pallas kernels  66.9 us (24%)
  between operations  13.8 us (5%)
  starting transfers between devices  6.01 us (2%)
  other arithmetic  5.11 us (2%)
  local copies, waits for them, and re-layouts  4.23 us (2%)
    reduce_scatter x1, waiting for transfers between devices, body(): lax.psum_scatter(part_var, ROW, scatter_dimension=0, tiled=True).astype(f32)  70.8 us
    reduce_scatter x1, waiting for transfers between devices, body(): lax.psum_scatter(part_theta, ROW, scatter_dimension=0, tiled=True)  44.6 us
    all_gather x1, waiting for transfers between devices, body(): sg = lax.all_gather(sg_own, ROW, axis=0, tiled=True)  38.2 us
    pallas_call x1, Pallas kernels, k3(): pl.pallas_call(k3_kernel, out_shape=(jax.ShapeDtypeStruct((t, ff), bf16),...  27.7 us
    pallas_call x1, Pallas kernels, k2(): pl.pallas_call(k2_kernel, out_shape=(jax.ShapeDtypeStruct((width, ff), bf...  25.7 us
    all_gather x1, waiting for transfers between devices, body(): th = lax.all_gather(th_own, ROW, axis=0, tiled=True)  23.6 us
    pallas_call x1, Pallas kernels, k1(): pl.pallas_call(k1_kernel, out_shape=(jax.ShapeDtypeStruct((width, cot.sha...  11.6 us
    all_to_all x1, starting transfers between devices, body(): arrived = lax.all_to_all(dx, 'col', split_axis=0, concat_axis=0, tiled=True)  5.85 us
  transfers between devices with their start and end apart: 5, of which 5 were waited for; matrix products, arithmetic and copies ran while one was open for 3% of the time, Pallas kernels for 24%

profile of v1, /device:TPU:1, one launch (start us, length us, event | category | flops | bytes accessed | tf_op | source)
XLA Modules:
  0.0 276.3 jit_solution(12782922953486601951)
XLA Ops:
  7.2 0.0 all-gather.5.cloned.1.call-start
  7.2 1.9 prep.1
  9.1 0.0 all-gather.5.cloned.1.call-update
  9.1 0.0 all-gather.3.cloned.1.call-start
  9.2 0.7 all-gather.3.cloned.1.call-update
  9.9 0.0 reduce-scatter.3.cloned.1.call-start
  9.9 1.4 copy.17.rows_ref
  11.3 11.6 %k1.1 = (bf16[1024,1536]{1,0:T(8,128)(2,1)}, bf16[32,128,512]{2,1,0:T(8,128)(2,1)}) custom-call(s32[12,8]{1,0:T(8,128)} %copy.17.rows_ref, bf16[512,4096]{1,0:T(8,128)(2,1)} %tok_ref.5, bf16[512,1536]{1,0:T(8,128)(2,1)} %cot_ref.5), custom_call_target="tpu_custom_call" | custom-call | tf_op jit(solution)/shard_map/k1/pallas_call | solution.py:50
  22.9 0.0 reduce-scatter.3.cloned.1.call-update
  22.9 0.0 reduce-scatter.5.cloned.1.call-start
  23.0 38.2 %all-gather.5.cloned.1.call-done.sg_ref = bf16[1024,1536]{1,0:T(8,128)(2,1)} async-done(((bf16[64,1536]{1,0:T(8,128)(2,1)}), bf16[1024,1536]{1,0:T(8,128)(2,1)}) %all-gather.5.cloned.1.call-update) | async-done | bytes 3145744 | tf_op jit(solution)/shard_map/all_gather | solution.py:128
  61.2 25.7 %k2.1 = (bf16[1024,1536]{1,0:T(8,128)(2,1)}, bf16[512,1536]{1,0:T(8,128)(2,1)}, f32[512,1536]{1,0:T(8,128)}) custom-call(s32[12,8]{1,0:T(8,128)} %copy.17.rows_ref, bf16[512,4096]{1,0:T(8,128)(2,1)} %tok_ref.5, bf16[32,128,512]{2,1,0:T(8,128)(2,1)} %get-tuple-element.15.tokT_ref, bf16[1024,1536]{1,0:T(8,128)(2,1)} %all-gather.5.cloned.1.call-done.sg_ref, ...), custom_call_target="tpu_custom_call" | custom-call | tf_op jit(solution)/shard_map/k2/pallas_call | solution.py:81
  86.9 0.0 reduce-scatter.5.cloned.1.call-update
  86.9 23.6 %all-gather.3.cloned.1.call-done.th_ref = bf16[1024,1536]{1,0:T(8,128)(2,1)} async-done(((bf16[64,1536]{1,0:T(8,128)(2,1)}), bf16[1024,1536]{1,0:T(8,128)(2,1)}) %all-gather.3.cloned.1.call-update) | async-done | bytes 3145744 | tf_op jit(solution)/shard_map/all_gather | solution.py:129
  110.5 27.7 %k3.1 = (bf16[512,1536]{1,0:T(8,128)(2,1)}, bf16[8,512,512]{2,1,0:T(8,128)(2,1)}) custom-call(s32[12,8]{1,0:T(8,128)} %copy.17.rows_ref, bf16[512,4096]{1,0:T(8,128)(2,1)} %tok_ref.5, bf16[1024,1536]{1,0:T(8,128)(2,1)} %all-gather.3.cloned.1.call-done.th_ref, bf16[1024,1536]{1,0:T(8,128)(2,1)} %all-gather.5.cloned.1.call-done.sg_ref, ...), custom_call_target="tpu_custom_call" | custom-call | tf_op jit(solution)/shard_map/k3/pallas_call | solution.py:119
  138.3 5.8 %all-to-all-start = ((bf16[8,512,512]{2,1,0:T(8,128)(2,1)}), bf16[8,512,512]{2,1,0:T(8,128)(2,1)}, u32[]{:S(2)}, u32[]{:S(2)}) async-start(bf16[8,512,512]{2,1,0:T(8,128)(2,1)} %get-tuple-element.19), calls=%async_computation | async-start | bytes 8388608 | tf_op jit(solution)/shard_map/all_to_all | solution.py:141
  144.1 44.6 %reduce-scatter.3.cloned.1.call-done = bf16[64,1536]{1,0:T(8,128)(2,1)} async-done(((bf16[1024,1536]{1,0:T(8,128)(2,1)}), bf16[64,1536]{1,0:T(8,128)(2,1)}) %reduce-scatter.3.cloned.1.call-update) | async-done | bytes 196624 | tf_op jit(solution)/shard_map/reduce_scatter | solution.py:133
  188.7 1.0 convert_multiply_fusion
  189.7 0.1 mul.23
  189.8 0.9 copy.19
  190.6 0.0 copy-start
  190.6 2.3 all-to-all-done
  192.9 3.8 %convert_reduce_fusion = f32[512,512]{1,0:T(8,128)} fusion(bf16[8,512,512]{2,1,0:T(8,128)(2,1)} %all-to-all-done), kind=kLoop, calls=%fused_computation | loop fusion | flops 3932160 | bytes 5242880 | tf_op jit(solution)/shard_map/reduce_sum | solution.py:142
  196.8 70.8 %reduce-scatter.5.cloned.1.call-done = bf16[64,1536]{1,0:T(8,128)(2,1)} async-done(((bf16[1024,1536]{1,0:T(8,128)(2,1)}), bf16[64,1536]{1,0:T(8,128)(2,1)}) %reduce-scatter.5.cloned.1.call-update) | async-done | bytes 196624 | tf_op jit(solution)/shard_map/reduce_scatter | solution.py:134
  267.5 1.1 reshape.16
  268.6 0.0 copy-done
  268.6 0.3 fusion
  268.9 0.9 copy.20
Async XLA Ops:
  7.2 54.0 %all-gather.5.cloned.1.call-start = ((), (), s32[]{:S(2)}) async-start(), calls=%async_computation.4 | async-start | bytes 3342336 | tf_op jit(solution)/shard_map/all_gather | solution.py:128
  9.1 101.4 %all-gather.3.cloned.1.call-start = ((), (), s32[]{:S(2)}) async-start(), calls=%async_computation.3 | async-start | bytes 3342336 | tf_op jit(solution)/shard_map/all_gather | solution.py:129
  9.9 178.8 %reduce-scatter.3.cloned.1.call-start = ((), (), s32[]{:S(2)}) async-start(), calls=%async_computation.5 | async-start | bytes 3342336 | tf_op jit(solution)/shard_map/reduce_scatter | solution.py:133
  22.9 244.6 %reduce-scatter.5.cloned.1.call-start = ((), (), s32[]{:S(2)}) async-start(), calls=%async_computation.6 | async-start | bytes 3342336 | tf_op jit(solution)/shard_map/reduce_scatter | solution.py:134
  138.3 54.7 %all-to-all-start = ((bf16[8,512,512]{2,1,0:T(8,128)(2,1)}), bf16[8,512,512]{2,1,0:T(8,128)(2,1)}, u32[]{:S(2)}, u32[]{:S(2)}) async-start(bf16[8,512,512]{2,1,0:T(8,128)(2,1)} %get-tuple-element.19), calls=%async_computation | async-start | bytes 8388608 | tf_op jit(solution)/shard_map/all_to_all | solution.py:141
  190.6 78.0 %copy-start = (f32[12,64,128]{2,1,0:T(8,128)S(1)}, f32[12,64,128]{2,1,0:T(8,128)}, u32[]{:S(2)}) copy-start(f32[12,64,128]{2,1,0:T(8,128)} %ls_ref.1) | copy-start | bytes 1179652
Sparse Core Ops, SparseCore 0:
  10.7 50.4 all-gather.4
  63.9 46.5 all-gather.2
  113.9 74.7 reduce-scatter.2
  191.9 75.6 reduce-scatter.4
